TPU v7x, 512 devices: a whole 4x4x16 slice. The times are simulated.
512 devices in a mesh: fsdp: 16 (over x, y), dp: 32 (over z, core).
Axes of the slice: x: 4, y: 4, z: 16, core: 2. Of those that a mesh axis runs over, the one named last changes fastest.
Arguments:
- tokens: bfloat16 [65536, 4096], P(('fsdp', 'dp')), may hold values from -6 to 6
- master_old: float32 [512, 128, 128], P(('fsdp', 'dp')), may hold values from -0.25 to 0.25
- moment_old: float32 [512, 128, 128], P(('fsdp', 'dp')), may hold values from -6 to 6
- second_old: float32 [512, 128, 128], P(('fsdp', 'dp')), may hold values from 0.01 to 1
- old_cell: int32 [112, 4], P('fsdp'), may hold values from 0 to 31, as said below
- new_cell: int32 [112, 4], P('fsdp'), may hold values from 0 to 31, as said below
- regrown: int32 [112, 4], P('fsdp'), may hold values 0 or 1
- new_rows: int32 [112, 4], replicated, may hold values from 0 to 31, as said below
Outputs:
- hidden: bfloat16 [65536, 14336], P(('fsdp', 'dp'))
- master_new: float32 [512, 128, 128], P(('fsdp', 'dp'))
- moment_new: float32 [512, 128, 128], P(('fsdp', 'dp'))
- second_new: float32 [512, 128, 128], P(('fsdp', 'dp'))
Inputs may be any that keep to these rules, and one draw needn't show every extreme that they name: `old_cell`: within one fsdp index, taking its slots column by column and then by k, the old cells strictly increase; a cell's index // 1 is its holder along dp and index % 1 its place in that holder's buffer. `new_cell`: strictly increasing in the same order; every slot's new cell differs from its old cell by at most 4, and by exactly 4 for some slot of every fsdp index. `new_rows`: the 4 block rows of one block column are distinct.
All inputs are finite; a program needn't handle non-finite values. No bound on the sum of `regrown` on one device may be relied on, other than what follows from the above.
Results may differ from a plain program's by a relative error of at most 0.007.
Values may be sent and summed in bfloat16 or wider, within the bound.
No kernel may reach another device: no remote copies, remote signals or barrier semaphores. Data moves between devices by JAX's collectives and lax.ppermute only.
A program may use at most 128 MiB of HBM per device.

v0:
```python
import jax
import jax.numpy as jnp
from jax import lax
from jax.sharding import PartitionSpec as P


def passed_along(block, axis, distance):
    devices = range(lax.axis_size(axis))
    route = [(i - distance, i) for i in devices if i - distance in devices]
    return lax.ppermute(block, axis, route)


def on_device(tokens, master_old, moment_old, second_old, old_cell, new_cell, regrown, new_rows):
    block_size = master_old.shape[1]
    capacity = master_old.shape[0]
    column_count = old_cell.shape[0]
    nonzero_count = old_cell.shape[1]
    slot_count = column_count * nonzero_count
    axis_width = lax.axis_size("dp")
    cell_count = axis_width * capacity
    farthest = min((cell_count - slot_count + capacity - 1) // capacity, axis_width - 1)
    holder = lax.axis_index("dp")
    old_flat = old_cell.reshape(-1)
    new_flat = new_cell.reshape(-1)
    keep_flag = regrown.reshape(-1) == 0
    my_cells = holder * capacity + jnp.arange(capacity, dtype=jnp.int32)
    matches = new_flat[None, :] == my_cells[:, None]
    present = jnp.any(matches & keep_flag[None, :], axis=1)
    source = jnp.sum(jnp.where(matches, old_flat[None, :], 0), axis=1)
    offset = holder - source // capacity
    slot_place = source % capacity
    candidate = jnp.where(offset > 0, 2 * offset - 1, jnp.where(offset < 0, -2 * offset, 0))
    pick_index = candidate * capacity + slot_place
    own_states = (master_old, moment_old, second_old)
    shift_list = []
    for distance in range(1, farthest + 1):
        shift_list.append(distance)
        shift_list.append(-distance)
    received_list = [own_states]
    for by_value in shift_list:
        received_list.append(
            (
                passed_along(own_states[0].astype(jnp.bfloat16), "dp", by_value).astype(
                    jnp.float32
                ),
                passed_along(own_states[1].astype(jnp.bfloat16), "dp", by_value).astype(
                    jnp.float32
                ),
                passed_along(own_states[2].astype(jnp.bfloat16), "dp", by_value).astype(
                    jnp.float32
                ),
            )
        )

    def settle(member):
        pool = jnp.concatenate([entry[member] for entry in received_list], axis=0)
        chosen = jnp.take(pool, pick_index, axis=0, mode="clip")
        return jnp.where(present[:, None, None], chosen, jnp.float32(0.0))

    master_new = settle(0)
    moment_new = settle(1)
    second_new = settle(2)
    cell_blocks = master_new.astype(jnp.bfloat16)
    group_cells = lax.all_gather(cell_blocks, "dp", axis=0, tiled=True)
    panel = jnp.take(group_cells, new_flat, axis=0).reshape(
        column_count, nonzero_count, block_size, block_size
    )
    token_count = tokens.shape[0]
    token_blocks = tokens.reshape(token_count, tokens.shape[1] // block_size, block_size)
    panel_piece = lax.all_gather(panel, "fsdp", axis=0, tiled=True)
    count = panel_piece.shape[0]
    picked = jnp.take(token_blocks, new_rows.reshape(-1), axis=1)
    picked = picked.reshape(token_count, count, nonzero_count, block_size)
    product = jnp.einsum("tcka,ckab->tcb", picked, panel_piece, preferred_element_type=jnp.float32)
    hidden = product.reshape(token_count, count * block_size).astype(jnp.bfloat16)
    return (hidden, master_new, moment_new, second_new)


def solution(mesh):
    return jax.shard_map(
        on_device,
        mesh=mesh,
        in_specs=(
            P(("fsdp", "dp"), None),
            P(("fsdp", "dp"), None, None),
            P(("fsdp", "dp"), None, None),
            P(("fsdp", "dp"), None, None),
            P("fsdp", None),
            P("fsdp", None),
            P("fsdp", None),
            P(),
        ),
        out_specs=(
            P(("fsdp", "dp"), None),
            P(("fsdp", "dp"), None, None),
            P(("fsdp", "dp"), None, None),
            P(("fsdp", "dp"), None, None),
        ),
        check_vma=False,
    )
```

profile of v0, /device:TPU:1, one launch (start us, length us, event | category | flops | bytes accessed | tf_op | source)
XLA Modules:
  0.0 264.1 jit_solution(16962180668199227297)
XLA Ops:
  8.1 4.9 %collective-permute-start = (bf16[1,128,128]{2,1,0:T(8,128)(2,1)S(1)}, bf16[1,128,128]{2,1,0:T(8,128)(2,1)S(1)}, u32[]{:S(2)}, u32[]{:S(2)}) collective-permute-start(bf16[1,128,128]{2,1,0:T(8,128)(2,1)S(1)} %get-tuple-element.61), channel_id=1, source_target_pairs={{0,1},{1,2},{2,3},{3,4},{4,5},{5,6},{6,7},{7,8},{8,9},{9,10},{10,1... | collective-permute-start | bytes 98312 | tf_op jit(solution)/shard_map/ppermute | solution.py:10
  13.1 5.1 %collective-permute-start.1 = (bf16[1,128,128]{2,1,0:T(8,128)(2,1)S(1)}, bf16[1,128,128]{2,1,0:T(8,128)(2,1)S(1)}, u32[]{:S(2)}, u32[]{:S(2)}) collective-permute-start(bf16[1,128,128]{2,1,0:T(8,128)(2,1)S(1)} %get-tuple-element.61), channel_id=1, source_target_pairs={{1,0},{2,1},{3,2},{4,3},{5,4},{6,5},{7,6},{8,7},{9,8},{10,9},{11,1... | collective-permute-start | bytes 98312 | tf_op jit(solution)/shard_map/ppermute | solution.py:10
  19.5 1.3 collective-permute-start.3
  20.8 5.0 %collective-permute-start.4 = (bf16[1,128,128]{2,1,0:T(8,128)(2,1)S(1)}, bf16[1,128,128]{2,1,0:T(8,128)(2,1)S(1)}, u32[]{:S(2)}, u32[]{:S(2)}) collective-permute-start(bf16[1,128,128]{2,1,0:T(8,128)(2,1)S(1)} %get-tuple-element.61), channel_id=1, source_target_pairs={{0,3},{1,4},{2,5},{3,6},{4,7},{5,8},{6,9},{7,10},{8,11},{9,12},{10... | collective-permute-start | bytes 98312 | tf_op jit(solution)/shard_map/ppermute | solution.py:10
  25.9 1.4 and_reduce_fusion
  27.3 1.3 select_reduce_fusion
  29.3 1.3 collective-permute-start.5
  30.6 9.2 %collective-permute-start.6 = (bf16[1,128,128]{2,1,0:T(8,128)(2,1)S(1)}, bf16[1,128,128]{2,1,0:T(8,128)(2,1)S(1)}, u32[]{:S(2)}, u32[]{:S(2)}) collective-permute-start(bf16[1,128,128]{2,1,0:T(8,128)(2,1)S(1)} %get-tuple-element.61), channel_id=1, source_target_pairs={{0,4},{1,5},{2,6},{3,7},{4,8},{5,9},{6,10},{7,11},{8,12},{9,13},{1... | collective-permute-start | bytes 98312 | tf_op jit(solution)/shard_map/ppermute | solution.py:10
  39.8 1.3 collective-permute-start.7
  41.2 4.1 %collective-permute-done.7 = bf16[1,128,128]{2,1,0:T(8,128)(2,1)S(1)} collective-permute-done((bf16[1,128,128]{2,1,0:T(8,128)(2,1)S(1)}, bf16[1,128,128]{2,1,0:T(8,128)(2,1)S(1)}, u32[]{:S(2)}, u32[]{:S(2)}) %collective-permute-start.7) | collective-permute-done | bytes 32800 | tf_op jit(solution)/shard_map/ppermute | solution.py:10
  47.7 73.8 %all-gather.3.cloned.1.call-done = bf16[32,128,128]{2,1,0:T(8,128)(2,1)} async-done(((bf16[1,128,128]{2,1,0:T(8,128)(2,1)}), bf16[32,128,128]{2,1,0:T(8,128)(2,1)}) %all-gather.3.cloned.1.call-update) | async-done | bytes 1048592 | tf_op jit(solution)/shard_map/all_gather | solution.py:64
  121.4 1.9 gather_fusion
  125.4 3.2 %collective-permute-start.16 = (bf16[1,128,128]{2,1,0:T(8,128)(2,1)S(1)}, bf16[1,128,128]{2,1,0:T(8,128)(2,1)S(1)}, u32[]{:S(2)}, u32[]{:S(2)}) collective-permute-start(bf16[1,128,128]{2,1,0:T(8,128)(2,1)S(1)} %get-tuple-element.57), channel_id=1, source_target_pairs={{0,1},{1,2},{2,3},{3,4},{4,5},{5,6},{6,7},{7,8},{8,9},{9,10},{10,1... | collective-permute-start | bytes 98312 | tf_op jit(solution)/shard_map/ppermute | solution.py:10
  128.6 1.9 collective-permute-start.17
  130.5 2.3 collective-permute-start.18
  132.8 1.3 collective-permute-start.19
  134.1 6.0 %collective-permute-start.20 = (bf16[1,128,128]{2,1,0:T(8,128)(2,1)S(1)}, bf16[1,128,128]{2,1,0:T(8,128)(2,1)S(1)}, u32[]{:S(2)}, u32[]{:S(2)}) collective-permute-start(bf16[1,128,128]{2,1,0:T(8,128)(2,1)S(1)} %get-tuple-element.57), channel_id=1, source_target_pairs={{0,3},{1,4},{2,5},{3,6},{4,7},{5,8},{6,9},{7,10},{8,11},{9,12},{10... | collective-permute-start | bytes 98312 | tf_op jit(solution)/shard_map/ppermute | solution.py:10
  142.7 1.6 copy.35
  145.1 13.3 %gather_fusion.1 = bf16[448,128,128]{2,1,0:T(8,128)(2,1)} fusion(bf16[128,32,128]{2,0,1:T(8,128)(2,1)S(1)} %copy.37, s32[1024]{0:T(1024)S(1)} %pad_clamp_fusion), kind=kCustom, calls=%fused_computation.1 | custom fusion | bytes 29361920 | tf_op jit(solution)/shard_map/jit(_take)/gather | solution.py:72
  159.7 6.6 %collective-permute-start.22 = (bf16[1,128,128]{2,1,0:T(8,128)(2,1)S(1)}, bf16[1,128,128]{2,1,0:T(8,128)(2,1)S(1)}, u32[]{:S(2)}, u32[]{:S(2)}) collective-permute-start(bf16[1,128,128]{2,1,0:T(8,128)(2,1)S(1)} %get-tuple-element.57), channel_id=1, source_target_pairs={{0,4},{1,5},{2,6},{3,7},{4,8},{5,9},{6,10},{7,11},{8,12},{9,13},{1... | collective-permute-start | bytes 98312 | tf_op jit(solution)/shard_map/ppermute | solution.py:10
  166.3 1.3 collective-permute-start.23
  167.6 2.2 collective-permute-start.8
  169.8 2.2 collective-permute-start.9
  172.0 6.4 %collective-permute-start.10 = (bf16[1,128,128]{2,1,0:T(8,128)(2,1)S(1)}, bf16[1,128,128]{2,1,0:T(8,128)(2,1)S(1)}, u32[]{:S(2)}, u32[]{:S(2)}) collective-permute-start(bf16[1,128,128]{2,1,0:T(8,128)(2,1)S(1)} %get-tuple-element.59), channel_id=1, source_target_pairs={{0,2},{1,3},{2,4},{3,5},{4,6},{5,7},{6,8},{7,9},{8,10},{9,11},{10,... | collective-permute-start | bytes 98312 | tf_op jit(solution)/shard_map/ppermute | solution.py:10
  178.5 1.3 collective-permute-start.11
  179.8 6.0 %collective-permute-start.12 = (bf16[1,128,128]{2,1,0:T(8,128)(2,1)S(1)}, bf16[1,128,128]{2,1,0:T(8,128)(2,1)S(1)}, u32[]{:S(2)}, u32[]{:S(2)}) collective-permute-start(bf16[1,128,128]{2,1,0:T(8,128)(2,1)S(1)} %get-tuple-element.59), channel_id=1, source_target_pairs={{0,3},{1,4},{2,5},{3,6},{4,7},{5,8},{6,9},{7,10},{8,11},{9,12},{10... | collective-permute-start | bytes 98312 | tf_op jit(solution)/shard_map/ppermute | solution.py:10
  185.9 1.3 collective-permute-start.13
  187.2 8.8 %collective-permute-start.14 = (bf16[1,128,128]{2,1,0:T(8,128)(2,1)S(1)}, bf16[1,128,128]{2,1,0:T(8,128)(2,1)S(1)}, u32[]{:S(2)}, u32[]{:S(2)}) collective-permute-start(bf16[1,128,128]{2,1,0:T(8,128)(2,1)S(1)} %get-tuple-element.59), channel_id=1, source_target_pairs={{0,4},{1,5},{2,6},{3,7},{4,8},{5,9},{6,10},{7,11},{8,12},{9,13},{1... | collective-permute-start | bytes 98312 | tf_op jit(solution)/shard_map/ppermute | solution.py:10
  198.7 3.3 %collective-permute-done.15 = bf16[1,128,128]{2,1,0:T(8,128)(2,1)S(1)} collective-permute-done((bf16[1,128,128]{2,1,0:T(8,128)(2,1)S(1)}, bf16[1,128,128]{2,1,0:T(8,128)(2,1)S(1)}, u32[]{:S(2)}, u32[]{:S(2)}) %collective-permute-start.15) | collective-permute-done | bytes 32800 | tf_op jit(solution)/shard_map/ppermute | solution.py:10
  203.3 34.5 %all-gather.5.cloned.1.call-done = bf16[112,4,128,128]{3,2,1,0:T(8,128)(2,1)} async-done(((bf16[7,4,128,128]{3,2,1,0:T(8,128)(2,1)}), bf16[112,4,128,128]{3,2,1,0:T(8,128)(2,1)}) %all-gather.5.cloned.1.call-update) | async-done | bytes 14680080 | tf_op jit(solution)/shard_map/all_gather | solution.py:70
  237.7 13.5 %bitcast_convert_fusion = bf16[112,128,128]{2,1,0:T(8,128)(2,1)} fusion(bf16[112,4,128,128]{3,2,1,0:T(8,128)(2,1)} %all-gather.5.cloned.1.call-done, bf16[128,112,4,128]{3,0,2,1:T(8,128)(2,1)} %bitcast.15, pred[112,4]{1,0:T(8,128)(4,1)S(1)} %copy.34), kind=kOutput, calls=%fused_computation.5 | convolution fusion | flops 1888223232 | bytes 33030592 | tf_op jit(solution)/shard_map/tcka,ckab->tcb/dot_general | solution.py:74
  251.2 6.1 %copy.39 = bf16[128,14336]{1,0:T(8,128)(2,1)} copy(bf16[128,14336]{0,1:T(8,128)(2,1)} %bitcast.17) | data formatting | bytes 7340032
  (72 shorter events, 15.2 us)
Async XLA Ops:
  7.2 114.3 %all-gather.3.cloned.1.call-start = ((), (), s32[]{:S(2)}) async-start(), calls=%async_computation | async-start | bytes 1081344 | tf_op jit(solution)/shard_map/all_gather | solution.py:64
  8.1 21.1 %collective-permute-start = (bf16[1,128,128]{2,1,0:T(8,128)(2,1)S(1)}, bf16[1,128,128]{2,1,0:T(8,128)(2,1)S(1)}, u32[]{:S(2)}, u32[]{:S(2)}) collective-permute-start(bf16[1,128,128]{2,1,0:T(8,128)(2,1)S(1)} %get-tuple-element.61), channel_id=1, source_target_pairs={{0,1},{1,2},{2,3},{3,4},{4,5},{5,6},{6,7},{7,8},{8,9},{9,10},{10,1... | collective-permute-start | bytes 98312 | tf_op jit(solution)/shard_map/ppermute | solution.py:10
  13.1 17.5 %collective-permute-start.1 = (bf16[1,128,128]{2,1,0:T(8,128)(2,1)S(1)}, bf16[1,128,128]{2,1,0:T(8,128)(2,1)S(1)}, u32[]{:S(2)}, u32[]{:S(2)}) collective-permute-start(bf16[1,128,128]{2,1,0:T(8,128)(2,1)S(1)} %get-tuple-element.61), channel_id=1, source_target_pairs={{1,0},{2,1},{3,2},{4,3},{5,4},{6,5},{7,6},{8,7},{9,8},{10,9},{11,1... | collective-permute-start | bytes 98312 | tf_op jit(solution)/shard_map/ppermute | solution.py:10
  18.2 21.5 %collective-permute-start.2 = (bf16[1,128,128]{2,1,0:T(8,128)(2,1)S(1)}, bf16[1,128,128]{2,1,0:T(8,128)(2,1)S(1)}, u32[]{:S(2)}, u32[]{:S(2)}) collective-permute-start(bf16[1,128,128]{2,1,0:T(8,128)(2,1)S(1)} %get-tuple-element.61), channel_id=1, source_target_pairs={{0,2},{1,3},{2,4},{3,5},{4,6},{5,7},{6,8},{7,9},{8,10},{9,11},{10,... | collective-permute-start | bytes 98312 | tf_op jit(solution)/shard_map/ppermute | solution.py:10
  19.5 21.6 %collective-permute-start.3 = (bf16[1,128,128]{2,1,0:T(8,128)(2,1)S(1)}, bf16[1,128,128]{2,1,0:T(8,128)(2,1)S(1)}, u32[]{:S(2)}, u32[]{:S(2)}) collective-permute-start(bf16[1,128,128]{2,1,0:T(8,128)(2,1)S(1)} %get-tuple-element.61), channel_id=1, source_target_pairs={{2,0},{3,1},{4,2},{5,3},{6,4},{7,5},{8,6},{9,7},{10,8},{11,9},{12,... | collective-permute-start | bytes 98312 | tf_op jit(solution)/shard_map/ppermute | solution.py:10
  20.8 20.3 %collective-permute-start.4 = (bf16[1,128,128]{2,1,0:T(8,128)(2,1)S(1)}, bf16[1,128,128]{2,1,0:T(8,128)(2,1)S(1)}, u32[]{:S(2)}, u32[]{:S(2)}) collective-permute-start(bf16[1,128,128]{2,1,0:T(8,128)(2,1)S(1)} %get-tuple-element.61), channel_id=1, source_target_pairs={{0,3},{1,4},{2,5},{3,6},{4,7},{5,8},{6,9},{7,10},{8,11},{9,12},{10... | collective-permute-start | bytes 98312 | tf_op jit(solution)/shard_map/ppermute | solution.py:10
  29.3 11.9 %collective-permute-start.5 = (bf16[1,128,128]{2,1,0:T(8,128)(2,1)S(1)}, bf16[1,128,128]{2,1,0:T(8,128)(2,1)S(1)}, u32[]{:S(2)}, u32[]{:S(2)}) collective-permute-start(bf16[1,128,128]{2,1,0:T(8,128)(2,1)S(1)} %get-tuple-element.61), channel_id=1, source_target_pairs={{3,0},{4,1},{5,2},{6,3},{7,4},{8,5},{9,6},{10,7},{11,8},{12,9},{13... | collective-permute-start | bytes 98312 | tf_op jit(solution)/shard_map/ppermute | solution.py:10
  30.6 10.6 %collective-permute-start.6 = (bf16[1,128,128]{2,1,0:T(8,128)(2,1)S(1)}, bf16[1,128,128]{2,1,0:T(8,128)(2,1)S(1)}, u32[]{:S(2)}, u32[]{:S(2)}) collective-permute-start(bf16[1,128,128]{2,1,0:T(8,128)(2,1)S(1)} %get-tuple-element.61), channel_id=1, source_target_pairs={{0,4},{1,5},{2,6},{3,7},{4,8},{5,9},{6,10},{7,11},{8,12},{9,13},{1... | collective-permute-start | bytes 98312 | tf_op jit(solution)/shard_map/ppermute | solution.py:10
  39.8 5.6 %collective-permute-start.7 = (bf16[1,128,128]{2,1,0:T(8,128)(2,1)S(1)}, bf16[1,128,128]{2,1,0:T(8,128)(2,1)S(1)}, u32[]{:S(2)}, u32[]{:S(2)}) collective-permute-start(bf16[1,128,128]{2,1,0:T(8,128)(2,1)S(1)} %get-tuple-element.61), channel_id=1, source_target_pairs={{4,0},{5,1},{6,2},{7,3},{8,4},{9,5},{10,6},{11,7},{12,8},{13,9},{1... | collective-permute-start | bytes 98312 | tf_op jit(solution)/shard_map/ppermute | solution.py:10
  46.6 191.1 %all-gather.5.cloned.1.call-start = ((), (), s32[]{:S(2)}) async-start(), calls=%async_computation.1 | async-start | bytes 15597568 | tf_op jit(solution)/shard_map/all_gather | solution.py:70
  125.4 32.9 %collective-permute-start.16 = (bf16[1,128,128]{2,1,0:T(8,128)(2,1)S(1)}, bf16[1,128,128]{2,1,0:T(8,128)(2,1)S(1)}, u32[]{:S(2)}, u32[]{:S(2)}) collective-permute-start(bf16[1,128,128]{2,1,0:T(8,128)(2,1)S(1)} %get-tuple-element.57), channel_id=1, source_target_pairs={{0,1},{1,2},{2,3},{3,4},{4,5},{5,6},{6,7},{7,8},{8,9},{9,10},{10,1... | collective-permute-start | bytes 98312 | tf_op jit(solution)/shard_map/ppermute | solution.py:10
  128.6 31.1 %collective-permute-start.17 = (bf16[1,128,128]{2,1,0:T(8,128)(2,1)S(1)}, bf16[1,128,128]{2,1,0:T(8,128)(2,1)S(1)}, u32[]{:S(2)}, u32[]{:S(2)}) collective-permute-start(bf16[1,128,128]{2,1,0:T(8,128)(2,1)S(1)} %get-tuple-element.57), channel_id=1, source_target_pairs={{1,0},{2,1},{3,2},{4,3},{5,4},{6,5},{7,6},{8,7},{9,8},{10,9},{11,1... | collective-permute-start | bytes 98312 | tf_op jit(solution)/shard_map/ppermute | solution.py:10
  130.5 35.8 %collective-permute-start.18 = (bf16[1,128,128]{2,1,0:T(8,128)(2,1)S(1)}, bf16[1,128,128]{2,1,0:T(8,128)(2,1)S(1)}, u32[]{:S(2)}, u32[]{:S(2)}) collective-permute-start(bf16[1,128,128]{2,1,0:T(8,128)(2,1)S(1)} %get-tuple-element.57), channel_id=1, source_target_pairs={{0,2},{1,3},{2,4},{3,5},{4,6},{5,7},{6,8},{7,9},{8,10},{9,11},{10,... | collective-permute-start | bytes 98312 | tf_op jit(solution)/shard_map/ppermute | solution.py:10
  132.8 34.8 %collective-permute-start.19 = (bf16[1,128,128]{2,1,0:T(8,128)(2,1)S(1)}, bf16[1,128,128]{2,1,0:T(8,128)(2,1)S(1)}, u32[]{:S(2)}, u32[]{:S(2)}) collective-permute-start(bf16[1,128,128]{2,1,0:T(8,128)(2,1)S(1)} %get-tuple-element.57), channel_id=1, source_target_pairs={{2,0},{3,1},{4,2},{5,3},{6,4},{7,5},{8,6},{9,7},{10,8},{11,9},{12,... | collective-permute-start | bytes 98312 | tf_op jit(solution)/shard_map/ppermute | solution.py:10
  134.1 35.7 %collective-permute-start.20 = (bf16[1,128,128]{2,1,0:T(8,128)(2,1)S(1)}, bf16[1,128,128]{2,1,0:T(8,128)(2,1)S(1)}, u32[]{:S(2)}, u32[]{:S(2)}) collective-permute-start(bf16[1,128,128]{2,1,0:T(8,128)(2,1)S(1)} %get-tuple-element.57), channel_id=1, source_target_pairs={{0,3},{1,4},{2,5},{3,6},{4,7},{5,8},{6,9},{7,10},{8,11},{9,12},{10... | collective-permute-start | bytes 98312 | tf_op jit(solution)/shard_map/ppermute | solution.py:10
  158.4 13.7 %collective-permute-start.21 = (bf16[1,128,128]{2,1,0:T(8,128)(2,1)S(1)}, bf16[1,128,128]{2,1,0:T(8,128)(2,1)S(1)}, u32[]{:S(2)}, u32[]{:S(2)}) collective-permute-start(bf16[1,128,128]{2,1,0:T(8,128)(2,1)S(1)} %get-tuple-element.57), channel_id=1, source_target_pairs={{3,0},{4,1},{5,2},{6,3},{7,4},{8,5},{9,6},{10,7},{11,8},{12,9},{13... | collective-permute-start | bytes 98312 | tf_op jit(solution)/shard_map/ppermute | solution.py:10
  159.7 18.8 %collective-permute-start.22 = (bf16[1,128,128]{2,1,0:T(8,128)(2,1)S(1)}, bf16[1,128,128]{2,1,0:T(8,128)(2,1)S(1)}, u32[]{:S(2)}, u32[]{:S(2)}) collective-permute-start(bf16[1,128,128]{2,1,0:T(8,128)(2,1)S(1)} %get-tuple-element.57), channel_id=1, source_target_pairs={{0,4},{1,5},{2,6},{3,7},{4,8},{5,9},{6,10},{7,11},{8,12},{9,13},{1... | collective-permute-start | bytes 98312 | tf_op jit(solution)/shard_map/ppermute | solution.py:10
  166.3 13.5 %collective-permute-start.23 = (bf16[1,128,128]{2,1,0:T(8,128)(2,1)S(1)}, bf16[1,128,128]{2,1,0:T(8,128)(2,1)S(1)}, u32[]{:S(2)}, u32[]{:S(2)}) collective-permute-start(bf16[1,128,128]{2,1,0:T(8,128)(2,1)S(1)} %get-tuple-element.57), channel_id=1, source_target_pairs={{4,0},{5,1},{6,2},{7,3},{8,4},{9,5},{10,6},{11,7},{12,8},{13,9},{1... | collective-permute-start | bytes 98312 | tf_op jit(solution)/shard_map/ppermute | solution.py:10
  167.6 18.2 %collective-permute-start.8 = (bf16[1,128,128]{2,1,0:T(8,128)(2,1)S(1)}, bf16[1,128,128]{2,1,0:T(8,128)(2,1)S(1)}, u32[]{:S(2)}, u32[]{:S(2)}) collective-permute-start(bf16[1,128,128]{2,1,0:T(8,128)(2,1)S(1)} %get-tuple-element.59), channel_id=1, source_target_pairs={{0,1},{1,2},{2,3},{3,4},{4,5},{5,6},{6,7},{7,8},{8,9},{9,10},{10,1... | collective-permute-start | bytes 98312 | tf_op jit(solution)/shard_map/ppermute | solution.py:10
  169.8 17.3 %collective-permute-start.9 = (bf16[1,128,128]{2,1,0:T(8,128)(2,1)S(1)}, bf16[1,128,128]{2,1,0:T(8,128)(2,1)S(1)}, u32[]{:S(2)}, u32[]{:S(2)}) collective-permute-start(bf16[1,128,128]{2,1,0:T(8,128)(2,1)S(1)} %get-tuple-element.59), channel_id=1, source_target_pairs={{1,0},{2,1},{3,2},{4,3},{5,4},{6,5},{7,6},{8,7},{9,8},{10,9},{11,1... | collective-permute-start | bytes 98312 | tf_op jit(solution)/shard_map/ppermute | solution.py:10
  172.0 24.0 %collective-permute-start.10 = (bf16[1,128,128]{2,1,0:T(8,128)(2,1)S(1)}, bf16[1,128,128]{2,1,0:T(8,128)(2,1)S(1)}, u32[]{:S(2)}, u32[]{:S(2)}) collective-permute-start(bf16[1,128,128]{2,1,0:T(8,128)(2,1)S(1)} %get-tuple-element.59), channel_id=1, source_target_pairs={{0,2},{1,3},{2,4},{3,5},{4,6},{5,7},{6,8},{7,9},{8,10},{9,11},{10,... | collective-permute-start | bytes 98312 | tf_op jit(solution)/shard_map/ppermute | solution.py:10
  178.5 18.8 %collective-permute-start.11 = (bf16[1,128,128]{2,1,0:T(8,128)(2,1)S(1)}, bf16[1,128,128]{2,1,0:T(8,128)(2,1)S(1)}, u32[]{:S(2)}, u32[]{:S(2)}) collective-permute-start(bf16[1,128,128]{2,1,0:T(8,128)(2,1)S(1)} %get-tuple-element.59), channel_id=1, source_target_pairs={{2,0},{3,1},{4,2},{5,3},{6,4},{7,5},{8,6},{9,7},{10,8},{11,9},{12,... | collective-permute-start | bytes 98312 | tf_op jit(solution)/shard_map/ppermute | solution.py:10
  179.8 17.5 %collective-permute-start.12 = (bf16[1,128,128]{2,1,0:T(8,128)(2,1)S(1)}, bf16[1,128,128]{2,1,0:T(8,128)(2,1)S(1)}, u32[]{:S(2)}, u32[]{:S(2)}) collective-permute-start(bf16[1,128,128]{2,1,0:T(8,128)(2,1)S(1)} %get-tuple-element.59), channel_id=1, source_target_pairs={{0,3},{1,4},{2,5},{3,6},{4,7},{5,8},{6,9},{7,10},{8,11},{9,12},{10... | collective-permute-start | bytes 98312 | tf_op jit(solution)/shard_map/ppermute | solution.py:10
  185.9 11.5 %collective-permute-start.13 = (bf16[1,128,128]{2,1,0:T(8,128)(2,1)S(1)}, bf16[1,128,128]{2,1,0:T(8,128)(2,1)S(1)}, u32[]{:S(2)}, u32[]{:S(2)}) collective-permute-start(bf16[1,128,128]{2,1,0:T(8,128)(2,1)S(1)} %get-tuple-element.59), channel_id=1, source_target_pairs={{3,0},{4,1},{5,2},{6,3},{7,4},{8,5},{9,6},{10,7},{11,8},{12,9},{13... | collective-permute-start | bytes 98312 | tf_op jit(solution)/shard_map/ppermute | solution.py:10
  187.2 10.2 %collective-permute-start.14 = (bf16[1,128,128]{2,1,0:T(8,128)(2,1)S(1)}, bf16[1,128,128]{2,1,0:T(8,128)(2,1)S(1)}, u32[]{:S(2)}, u32[]{:S(2)}) collective-permute-start(bf16[1,128,128]{2,1,0:T(8,128)(2,1)S(1)} %get-tuple-element.59), channel_id=1, source_target_pairs={{0,4},{1,5},{2,6},{3,7},{4,8},{5,9},{6,10},{7,11},{8,12},{9,13},{1... | collective-permute-start | bytes 98312 | tf_op jit(solution)/shard_map/ppermute | solution.py:10
  196.0 6.0 %collective-permute-start.15 = (bf16[1,128,128]{2,1,0:T(8,128)(2,1)S(1)}, bf16[1,128,128]{2,1,0:T(8,128)(2,1)S(1)}, u32[]{:S(2)}, u32[]{:S(2)}) collective-permute-start(bf16[1,128,128]{2,1,0:T(8,128)(2,1)S(1)} %get-tuple-element.59), channel_id=1, source_target_pairs={{4,0},{5,1},{6,2},{7,3},{8,4},{9,5},{10,6},{11,7},{12,8},{13,9},{1... | collective-permute-start | bytes 98312 | tf_op jit(solution)/shard_map/ppermute | solution.py:10
Sparse Core Ops, SparseCore 0:
  46.8 74.6 all-gather.2
  125.1 112.6 all-gather.4
where the time goes:
time: 265 us; the launch traced here: 264 us
  waiting for transfers between devices  116 us (44%)
  starting transfers between devices  82.8 us (31%)
  local copies, waits for them, and re-layouts  25.5 us (10%)
  between operations  15.3 us (6%)
  matrix products  13.5 us (5%)
  other arithmetic  11.3 us (4%)
    ppermute x24, starting transfers between devices, passed_along(): return lax.ppermute(block, axis, route)  82.7 us
    all_gather x1, waiting for transfers between devices, on_device(): group_cells = lax.all_gather(cell_blocks, 'dp', axis=0, tiled=True)  73.8 us
    all_gather x1, waiting for transfers between devices, on_device(): panel_piece = lax.all_gather(panel, 'fsdp', axis=0, tiled=True)  34.5 us
    dot_general x1, matrix products, on_device(): jnp.einsum('tcka,ckab->tcb', picked, panel_piece, preferred_element_type=...  13.5 us
    gather x1, local copies, waits for them, and re-layouts, on_device(): picked = jnp.take(token_blocks, new_rows.reshape(-1), axis=1)  13.3 us
    unnamed x4, local copies, waits for them, and re-layouts  9.25 us
    ppermute x24, waiting for transfers between devices, passed_along(): return lax.ppermute(block, axis, route)  7.47 us
  transfers between devices with their start and end apart: 26, of which 4 were waited for; matrix products, arithmetic and copies ran while one was open for 10% of the time, Pallas kernels for 0%

commit v1 on v0

--- a/solution.py
+++ b/solution.py
@@ -2,6 +2,24 @@
 import jax.numpy as jnp
 from jax import lax
 from jax.sharding import PartitionSpec as P
+
+
+def ring_gather(value, axis, dim):
+    ways, here, hop = (lax.axis_size(axis), lax.axis_index(axis), value.shape[dim])
+    dims = [n * ways if d == dim else n for d, n in enumerate(value.shape)]
+    full = lax.dynamic_update_slice_in_dim(
+        jnp.zeros(dims, value.dtype), value, here * hop, axis=dim
+    )
+    going_up = going_down = value
+    for far in range(1, ways // 2 + 1):
+        going_up = lax.ppermute(going_up, axis, [(d, (d + 1) % ways) for d in range(ways)])
+        full = lax.dynamic_update_slice_in_dim(full, going_up, (here - far) % ways * hop, axis=dim)
+        if 2 * far < ways:
+            going_down = lax.ppermute(going_down, axis, [(d, (d - 1) % ways) for d in range(ways)])
+            full = lax.dynamic_update_slice_in_dim(
+                full, going_down, (here + far) % ways * hop, axis=dim
+            )
+    return full
 
 
 def passed_along(block, axis, distance):
@@ -67,7 +85,7 @@
     )
     token_count = tokens.shape[0]
     token_blocks = tokens.reshape(token_count, tokens.shape[1] // block_size, block_size)
-    panel_piece = lax.all_gather(panel, "fsdp", axis=0, tiled=True)
+    panel_piece = ring_gather(panel, "fsdp", 0)
     count = panel_piece.shape[0]
     picked = jnp.take(token_blocks, new_rows.reshape(-1), axis=1)
     picked = picked.reshape(token_count, count, nonzero_count, block_size)

time: 265 us -> 388 us (1.46)
  starting transfers between devices: 82.8 us -> 148 us
  local copies, waits for them, and re-layouts: 25.5 us -> 53.7 us
  waiting for transfers between devices: 116 us -> 140 us
  other arithmetic: 11.3 us -> 16 us
    ppermute x0 -> x15, starting transfers between devices: none -> 64.3 us  [the longest x7 47.6 us: ring_gather(): lax.ppermute(going_down, axis, [(d, (d - 1) % ways) for d in range(ways)])]
    ppermute x0 -> x15, waiting for transfers between devices: none -> 62.1 us  [the longest x8 34.8 us: ring_gather(): lax.ppermute(going_up, axis, [(d, (d + 1) % ways) for d in range(ways)])]
    all_gather x1 -> x0, waiting for transfers between devices: 34.5 us -> none  [on_device(): panel_piece = lax.all_gather(panel, 'fsdp', axis=0, tiled=True)]
    dynamic_update_slice x0 -> x15, local copies, waits for them, and re-layouts: none -> 20.1 us  [the longest x8 10.7 us: ring_gather(): lax.dynamic_update_slice_in_dim(full, going_up, (here - far) % ways * hop...]
    broadcast_in_dim x0 -> x1, local copies, waits for them, and re-layouts: none -> 8.92 us  [ring_gather(): jnp.zeros(dims, value.dtype)]
    unnamed x21, other arithmetic: 0.17 us -> 4.52 us
    unnamed x4 -> x18, local copies, waits for them, and re-layouts: 9.25 us -> 7.64 us
  transfers between devices with their start and end apart: 26 -> 40, of which waited for: 4 -> 9; matrix products, arithmetic and copies ran while one was open for 10% -> 12% of each run, Pallas kernels for 0% -> 0%
where the time goes in v1:
time: 388 us; the launch traced here: 386 us
  starting transfers between devices  148 us (38%)
  waiting for transfers between devices  140 us (36%)
  local copies, waits for them, and re-layouts  53.7 us (14%)
  other arithmetic  16 us (4%)
  between operations  15.5 us (4%)
  matrix products  13.4 us (3%)
    ppermute x24, starting transfers between devices, passed_along(): return lax.ppermute(block, axis, route)  83.4 us
    all_gather x1, waiting for transfers between devices, on_device(): group_cells = lax.all_gather(cell_blocks, 'dp', axis=0, tiled=True)  73.8 us
    ppermute x7, starting transfers between devices, ring_gather(): lax.ppermute(going_down, axis, [(d, (d - 1) % ways) for d in range(ways)])  47.6 us
    ppermute x8, waiting for transfers between devices, ring_gather(): lax.ppermute(going_up, axis, [(d, (d + 1) % ways) for d in range(ways)])  34.8 us
    ppermute x7, waiting for transfers between devices, ring_gather(): lax.ppermute(going_down, axis, [(d, (d - 1) % ways) for d in range(ways)])  27.3 us
    ppermute x8, starting transfers between devices, ring_gather(): lax.ppermute(going_up, axis, [(d, (d + 1) % ways) for d in range(ways)])  16.7 us
    dot_general x1, matrix products, on_device(): jnp.einsum('tcka,ckab->tcb', picked, panel_piece, preferred_element_type=...  13.4 us
    gather x1, local copies, waits for them, and re-layouts, on_device(): picked = jnp.take(token_blocks, new_rows.reshape(-1), axis=1)  13.4 us
  transfers between devices with their start and end apart: 40, of which 9 were waited for; matrix products, arithmetic and copies ran while one was open for 12% of the time, Pallas kernels for 0%

profile of v1, /device:TPU:1, one launch (start us, length us, event | category | flops | bytes accessed | tf_op | source)
XLA Modules:
  0.0 386.5 jit_solution(17579673034865341144)
XLA Ops:
  8.2 4.9 %collective-permute-start = (bf16[1,128,128]{2,1,0:T(8,128)(2,1)S(1)}, bf16[1,128,128]{2,1,0:T(8,128)(2,1)S(1)}, u32[]{:S(2)}, u32[]{:S(2)}) collective-permute-start(bf16[1,128,128]{2,1,0:T(8,128)(2,1)S(1)} %get-tuple-element.63), channel_id=1, source_target_pairs={{0,1},{1,2},{2,3},{3,4},{4,5},{5,6},{6,7},{7,8},{8,9},{9,10},{10,1... | collective-permute-start | bytes 98312 | tf_op jit(solution)/shard_map/ppermute | solution.py:28
  13.2 5.1 %collective-permute-start.1 = (bf16[1,128,128]{2,1,0:T(8,128)(2,1)S(1)}, bf16[1,128,128]{2,1,0:T(8,128)(2,1)S(1)}, u32[]{:S(2)}, u32[]{:S(2)}) collective-permute-start(bf16[1,128,128]{2,1,0:T(8,128)(2,1)S(1)} %get-tuple-element.63), channel_id=1, source_target_pairs={{1,0},{2,1},{3,2},{4,3},{5,4},{6,5},{7,6},{8,7},{9,8},{10,9},{11,1... | collective-permute-start | bytes 98312 | tf_op jit(solution)/shard_map/ppermute | solution.py:28
  20.9 5.0 %collective-permute-start.4 = (bf16[1,128,128]{2,1,0:T(8,128)(2,1)S(1)}, bf16[1,128,128]{2,1,0:T(8,128)(2,1)S(1)}, u32[]{:S(2)}, u32[]{:S(2)}) collective-permute-start(bf16[1,128,128]{2,1,0:T(8,128)(2,1)S(1)} %get-tuple-element.63), channel_id=1, source_target_pairs={{0,3},{1,4},{2,5},{3,6},{4,7},{5,8},{6,9},{7,10},{8,11},{9,12},{10... | collective-permute-start | bytes 98312 | tf_op jit(solution)/shard_map/ppermute | solution.py:28
  30.6 9.2 %collective-permute-start.6 = (bf16[1,128,128]{2,1,0:T(8,128)(2,1)S(1)}, bf16[1,128,128]{2,1,0:T(8,128)(2,1)S(1)}, u32[]{:S(2)}, u32[]{:S(2)}) collective-permute-start(bf16[1,128,128]{2,1,0:T(8,128)(2,1)S(1)} %get-tuple-element.63), channel_id=1, source_target_pairs={{0,4},{1,5},{2,6},{3,7},{4,8},{5,9},{6,10},{7,11},{8,12},{9,13},{1... | collective-permute-start | bytes 98312 | tf_op jit(solution)/shard_map/ppermute | solution.py:28
  41.3 4.1 %collective-permute-done.7 = bf16[1,128,128]{2,1,0:T(8,128)(2,1)S(1)} collective-permute-done((bf16[1,128,128]{2,1,0:T(8,128)(2,1)S(1)}, bf16[1,128,128]{2,1,0:T(8,128)(2,1)S(1)}, u32[]{:S(2)}, u32[]{:S(2)}) %collective-permute-start.7) | collective-permute-done | bytes 32800 | tf_op jit(solution)/shard_map/ppermute | solution.py:28
  47.7 73.8 %all-gather.2.cloned.1.call-done = bf16[32,128,128]{2,1,0:T(8,128)(2,1)} async-done(((bf16[1,128,128]{2,1,0:T(8,128)(2,1)}), bf16[32,128,128]{2,1,0:T(8,128)(2,1)}) %all-gather.2.cloned.1.call-update) | async-done | bytes 1048592 | tf_op jit(solution)/shard_map/all_gather | solution.py:82
  124.0 8.9 %broadcast_in_dim.57 = bf16[112,4,128,128]{2,3,1,0:T(8,128)(2,1)} broadcast(bf16[]{:T(256)} %constant.154.clone.1), dimensions={} | broadcast | bytes 14680066 | tf_op jit(solution)/shard_map/broadcast_in_dim | solution.py:11
  134.2 3.1 collective-permute-start.8
  137.3 5.5 %collective-permute-start.9 = (bf16[7,4,128,128]{2,3,1,0:T(8,128)(2,1)S(1)}, bf16[7,4,128,128]{2,3,1,0:T(8,128)(2,1)}, u32[]{:S(2)}, u32[]{:S(2)}) collective-permute-start(bf16[7,4,128,128]{2,3,1,0:T(8,128)(2,1)S(1)} %get-tuple-element.54), channel_id=1, source_target_pairs={{0,480},{32,0},{64,32},{96,64},{128,96},{160,128},{192,160},{224,1... | collective-permute-start | bytes 2752520 | tf_op jit(solution)/shard_map/ppermute | solution.py:18
  142.8 18.3 %collective-permute-done.8 = bf16[7,4,128,128]{2,3,1,0:T(8,128)(2,1)S(1)} collective-permute-done((bf16[7,4,128,128]{2,3,1,0:T(8,128)(2,1)S(1)}, bf16[7,4,128,128]{2,3,1,0:T(8,128)(2,1)S(1)}, u32[]{:S(2)}, u32[]{:S(2)}) %collective-permute-start.8) | collective-permute-done | bytes 917536 | tf_op jit(solution)/shard_map/ppermute | solution.py:15
  163.6 4.0 %collective-permute-start.31 = (bf16[1,128,128]{2,1,0:T(8,128)(2,1)S(1)}, bf16[1,128,128]{2,1,0:T(8,128)(2,1)S(1)}, u32[]{:S(2)}, u32[]{:S(2)}) collective-permute-start(bf16[1,128,128]{2,1,0:T(8,128)(2,1)S(1)} %get-tuple-element.59), channel_id=1, source_target_pairs={{0,1},{1,2},{2,3},{3,4},{4,5},{5,6},{6,7},{7,8},{8,9},{9,10},{10,1... | collective-permute-start | bytes 98312 | tf_op jit(solution)/shard_map/ppermute | solution.py:28
  169.6 2.3 collective-permute-start.33
  172.1 7.0 %collective-permute-start.11 = (bf16[7,4,128,128]{2,3,1,0:T(8,128)(2,1)}, bf16[7,4,128,128]{2,3,1,0:T(8,128)(2,1)}, u32[]{:S(2)}, u32[]{:S(2)}) collective-permute-start(bf16[7,4,128,128]{2,3,1,0:T(8,128)(2,1)} %collective-permute-done.9), channel_id=1, source_target_pairs={{0,480},{32,0},{64,32},{96,64},{128,96},{160,128},{192,160},{224,1... | collective-permute-start | bytes 2752520 | tf_op jit(solution)/shard_map/ppermute | solution.py:18
  179.1 8.1 %collective-permute-done.10 = bf16[7,4,128,128]{2,3,1,0:T(8,128)(2,1)} collective-permute-done((bf16[7,4,128,128]{2,3,1,0:T(8,128)(2,1)S(1)}, bf16[7,4,128,128]{2,3,1,0:T(8,128)(2,1)}, u32[]{:S(2)}, u32[]{:S(2)}) %collective-permute-start.10) | collective-permute-done | bytes 917536 | tf_op jit(solution)/shard_map/ppermute | solution.py:15
  191.3 13.4 %gather_fusion.1 = bf16[448,128,128]{2,1,0:T(8,128)(2,1)} fusion(bf16[128,32,128]{2,0,1:T(8,128)(2,1)S(1)} %copy.38, s32[1024]{0:T(1024)S(1)} %pad_clamp_fusion), kind=kCustom, calls=%fused_computation.1 | custom fusion | bytes 29361920 | tf_op jit(solution)/shard_map/jit(_take)/gather | solution.py:90
  206.6 7.0 %collective-permute-start.35 = (bf16[1,128,128]{2,1,0:T(8,128)(2,1)S(1)}, bf16[1,128,128]{2,1,0:T(8,128)(2,1)S(1)}, u32[]{:S(2)}, u32[]{:S(2)}) collective-permute-start(bf16[1,128,128]{2,1,0:T(8,128)(2,1)S(1)} %get-tuple-element.59), channel_id=1, source_target_pairs={{0,3},{1,4},{2,5},{3,6},{4,7},{5,8},{6,9},{7,10},{8,11},{9,12},{10... | collective-permute-start | bytes 98312 | tf_op jit(solution)/shard_map/ppermute | solution.py:28
  215.5 7.0 %collective-permute-start.13 = (bf16[7,4,128,128]{2,3,1,0:T(8,128)(2,1)}, bf16[7,4,128,128]{2,3,1,0:T(8,128)(2,1)S(1)}, u32[]{:S(2)}, u32[]{:S(2)}) collective-permute-start(bf16[7,4,128,128]{2,3,1,0:T(8,128)(2,1)} %collective-permute-done.11), channel_id=1, source_target_pairs={{0,480},{32,0},{64,32},{96,64},{128,96},{160,128},{192,160},{224,1... | collective-permute-start | bytes 2752520 | tf_op jit(solution)/shard_map/ppermute | solution.py:18
  225.1 5.0 %collective-permute-start.37 = (bf16[1,128,128]{2,1,0:T(8,128)(2,1)S(1)}, bf16[1,128,128]{2,1,0:T(8,128)(2,1)S(1)}, u32[]{:S(2)}, u32[]{:S(2)}) collective-permute-start(bf16[1,128,128]{2,1,0:T(8,128)(2,1)S(1)} %get-tuple-element.59), channel_id=1, source_target_pairs={{0,4},{1,5},{2,6},{3,7},{4,8},{5,9},{6,10},{7,11},{8,12},{9,13},{1... | collective-permute-start | bytes 98312 | tf_op jit(solution)/shard_map/ppermute | solution.py:28
  232.6 3.0 collective-permute-start.23
  238.8 6.1 %collective-permute-start.25 = (bf16[1,128,128]{2,1,0:T(8,128)(2,1)S(1)}, bf16[1,128,128]{2,1,0:T(8,128)(2,1)S(1)}, u32[]{:S(2)}, u32[]{:S(2)}) collective-permute-start(bf16[1,128,128]{2,1,0:T(8,128)(2,1)S(1)} %get-tuple-element.61), channel_id=1, source_target_pairs={{0,2},{1,3},{2,4},{3,5},{4,6},{5,7},{6,8},{7,9},{8,10},{9,11},{10,... | collective-permute-start | bytes 98312 | tf_op jit(solution)/shard_map/ppermute | solution.py:28
  244.9 7.0 %collective-permute-start.15 = (bf16[7,4,128,128]{2,3,1,0:T(8,128)(2,1)S(1)}, bf16[7,4,128,128]{2,3,1,0:T(8,128)(2,1)S(1)}, u32[]{:S(2)}, u32[]{:S(2)}) collective-permute-start(bf16[7,4,128,128]{2,3,1,0:T(8,128)(2,1)S(1)} %collective-permute-done.13), channel_id=1, source_target_pairs={{0,480},{32,0},{64,32},{96,64},{128,96},{160,128},{192,160},{224,1... | collective-permute-start | bytes 2752520 | tf_op jit(solution)/shard_map/ppermute | solution.py:18
  255.8 6.3 %collective-permute-start.27 = (bf16[1,128,128]{2,1,0:T(8,128)(2,1)S(1)}, bf16[1,128,128]{2,1,0:T(8,128)(2,1)S(1)}, u32[]{:S(2)}, u32[]{:S(2)}) collective-permute-start(bf16[1,128,128]{2,1,0:T(8,128)(2,1)S(1)} %get-tuple-element.61), channel_id=1, source_target_pairs={{0,3},{1,4},{2,5},{3,6},{4,7},{5,8},{6,9},{7,10},{8,11},{9,12},{10... | collective-permute-start | bytes 98312 | tf_op jit(solution)/shard_map/ppermute | solution.py:28
  263.4 8.8 %collective-permute-start.29 = (bf16[1,128,128]{2,1,0:T(8,128)(2,1)S(1)}, bf16[1,128,128]{2,1,0:T(8,128)(2,1)S(1)}, u32[]{:S(2)}, u32[]{:S(2)}) collective-permute-start(bf16[1,128,128]{2,1,0:T(8,128)(2,1)S(1)} %get-tuple-element.61), channel_id=1, source_target_pairs={{0,4},{1,5},{2,6},{3,7},{4,8},{5,9},{6,10},{7,11},{8,12},{9,13},{1... | collective-permute-start | bytes 98312 | tf_op jit(solution)/shard_map/ppermute | solution.py:28
  273.6 7.0 %collective-permute-start.17 = (bf16[7,4,128,128]{2,3,1,0:T(8,128)(2,1)S(1)}, bf16[7,4,128,128]{2,3,1,0:T(8,128)(2,1)S(1)}, u32[]{:S(2)}, u32[]{:S(2)}) collective-permute-start(bf16[7,4,128,128]{2,3,1,0:T(8,128)(2,1)S(1)} %collective-permute-done.15), channel_id=1, source_target_pairs={{0,480},{32,0},{64,32},{96,64},{128,96},{160,128},{192,160},{224,1... | collective-permute-start | bytes 2752520 | tf_op jit(solution)/shard_map/ppermute | solution.py:18
  284.7 13.2 %collective-permute-done.17 = bf16[7,4,128,128]{2,3,1,0:T(8,128)(2,1)S(1)} collective-permute-done((bf16[7,4,128,128]{2,3,1,0:T(8,128)(2,1)S(1)}, bf16[7,4,128,128]{2,3,1,0:T(8,128)(2,1)S(1)}, u32[]{:S(2)}, u32[]{:S(2)}) %collective-permute-start.17) | collective-permute-done | bytes 917536 | tf_op jit(solution)/shard_map/ppermute | solution.py:18
  297.9 7.1 %collective-permute-start.19 = (bf16[7,4,128,128]{2,3,1,0:T(8,128)(2,1)S(1)}, bf16[7,4,128,128]{2,3,1,0:T(8,128)(2,1)S(1)}, u32[]{:S(2)}, u32[]{:S(2)}) collective-permute-start(bf16[7,4,128,128]{2,3,1,0:T(8,128)(2,1)S(1)} %collective-permute-done.17), channel_id=1, source_target_pairs={{0,480},{32,0},{64,32},{96,64},{128,96},{160,128},{192,160},{224,1... | collective-permute-start | bytes 2752520 | tf_op jit(solution)/shard_map/ppermute | solution.py:18
  319.2 4.3 %collective-permute-done.19 = bf16[7,4,128,128]{2,3,1,0:T(8,128)(2,1)S(1)} collective-permute-done((bf16[7,4,128,128]{2,3,1,0:T(8,128)(2,1)S(1)}, bf16[7,4,128,128]{2,3,1,0:T(8,128)(2,1)S(1)}, u32[]{:S(2)}, u32[]{:S(2)}) %collective-permute-start.19) | collective-permute-done | bytes 917536 | tf_op jit(solution)/shard_map/ppermute | solution.py:18
  323.5 7.1 %collective-permute-start.21 = (bf16[7,4,128,128]{2,3,1,0:T(8,128)(2,1)S(1)}, bf16[7,4,128,128]{2,3,1,0:T(8,128)(2,1)S(1)}, u32[]{:S(2)}, u32[]{:S(2)}) collective-permute-start(bf16[7,4,128,128]{2,3,1,0:T(8,128)(2,1)S(1)} %collective-permute-done.19), channel_id=1, source_target_pairs={{0,480},{32,0},{64,32},{96,64},{128,96},{160,128},{192,160},{224,1... | collective-permute-start | bytes 2752520 | tf_op jit(solution)/shard_map/ppermute | solution.py:18
  340.4 9.8 %collective-permute-done.21 = bf16[7,4,128,128]{2,3,1,0:T(8,128)(2,1)S(1)} collective-permute-done((bf16[7,4,128,128]{2,3,1,0:T(8,128)(2,1)S(1)}, bf16[7,4,128,128]{2,3,1,0:T(8,128)(2,1)S(1)}, u32[]{:S(2)}, u32[]{:S(2)}) %collective-permute-start.21) | collective-permute-done | bytes 917536 | tf_op jit(solution)/shard_map/ppermute | solution.py:18
  351.2 7.9 %collective-permute-done.22 = bf16[7,4,128,128]{2,3,1,0:T(8,128)(2,1)S(1)} collective-permute-done((bf16[7,4,128,128]{2,3,1,0:T(8,128)(2,1)S(1)}, bf16[7,4,128,128]{2,3,1,0:T(8,128)(2,1)S(1)}, u32[]{:S(2)}, u32[]{:S(2)}) %collective-permute-start.22) | collective-permute-done | bytes 917536 | tf_op jit(solution)/shard_map/ppermute | solution.py:15
  360.1 13.4 %bitcast_convert_fusion = bf16[112,128,128]{2,1,0:T(8,128)(2,1)} fusion(bf16[112,4,128,128]{2,3,1,0:T(8,128)(2,1)} %constant_dynamic-update-slice_fusion.3, bf16[128,112,4,128]{3,0,2,1:T(8,128)(2,1)} %bitcast.15, pred[112,4]{1,0:T(8,128)(4,1)S(1)} %copy.35), kind=kOutput, calls=%fused_computation.5 | convolution fusion | flops 1888223232 | bytes 33030592 | tf_op jit(solution)/shard_map/tcka,ckab->tcb/dot_general | solution.py:92
  373.5 6.1 %copy.39 = bf16[128,14336]{1,0:T(8,128)(2,1)} copy(bf16[128,14336]{0,1:T(8,128)(2,1)} %bitcast.17) | data formatting | bytes 7340032
  (130 shorter events, 72.4 us)
Async XLA Ops:
  7.2 114.2 %all-gather.2.cloned.1.call-start = ((), (), s32[]{:S(2)}) async-start(), calls=%async_computation | async-start | bytes 1081344 | tf_op jit(solution)/shard_map/all_gather | solution.py:82
  8.2 21.1 %collective-permute-start = (bf16[1,128,128]{2,1,0:T(8,128)(2,1)S(1)}, bf16[1,128,128]{2,1,0:T(8,128)(2,1)S(1)}, u32[]{:S(2)}, u32[]{:S(2)}) collective-permute-start(bf16[1,128,128]{2,1,0:T(8,128)(2,1)S(1)} %get-tuple-element.63), channel_id=1, source_target_pairs={{0,1},{1,2},{2,3},{3,4},{4,5},{5,6},{6,7},{7,8},{8,9},{9,10},{10,1... | collective-permute-start | bytes 98312 | tf_op jit(solution)/shard_map/ppermute | solution.py:28
  13.2 17.5 %collective-permute-start.1 = (bf16[1,128,128]{2,1,0:T(8,128)(2,1)S(1)}, bf16[1,128,128]{2,1,0:T(8,128)(2,1)S(1)}, u32[]{:S(2)}, u32[]{:S(2)}) collective-permute-start(bf16[1,128,128]{2,1,0:T(8,128)(2,1)S(1)} %get-tuple-element.63), channel_id=1, source_target_pairs={{1,0},{2,1},{3,2},{4,3},{5,4},{6,5},{7,6},{8,7},{9,8},{10,9},{11,1... | collective-permute-start | bytes 98312 | tf_op jit(solution)/shard_map/ppermute | solution.py:28
  18.3 21.5 %collective-permute-start.2 = (bf16[1,128,128]{2,1,0:T(8,128)(2,1)S(1)}, bf16[1,128,128]{2,1,0:T(8,128)(2,1)S(1)}, u32[]{:S(2)}, u32[]{:S(2)}) collective-permute-start(bf16[1,128,128]{2,1,0:T(8,128)(2,1)S(1)} %get-tuple-element.63), channel_id=1, source_target_pairs={{0,2},{1,3},{2,4},{3,5},{4,6},{5,7},{6,8},{7,9},{8,10},{9,11},{10,... | collective-permute-start | bytes 98312 | tf_op jit(solution)/shard_map/ppermute | solution.py:28
  19.6 21.5 %collective-permute-start.3 = (bf16[1,128,128]{2,1,0:T(8,128)(2,1)S(1)}, bf16[1,128,128]{2,1,0:T(8,128)(2,1)S(1)}, u32[]{:S(2)}, u32[]{:S(2)}) collective-permute-start(bf16[1,128,128]{2,1,0:T(8,128)(2,1)S(1)} %get-tuple-element.63), channel_id=1, source_target_pairs={{2,0},{3,1},{4,2},{5,3},{6,4},{7,5},{8,6},{9,7},{10,8},{11,9},{12,... | collective-permute-start | bytes 98312 | tf_op jit(solution)/shard_map/ppermute | solution.py:28
  20.9 20.3 %collective-permute-start.4 = (bf16[1,128,128]{2,1,0:T(8,128)(2,1)S(1)}, bf16[1,128,128]{2,1,0:T(8,128)(2,1)S(1)}, u32[]{:S(2)}, u32[]{:S(2)}) collective-permute-start(bf16[1,128,128]{2,1,0:T(8,128)(2,1)S(1)} %get-tuple-element.63), channel_id=1, source_target_pairs={{0,3},{1,4},{2,5},{3,6},{4,7},{5,8},{6,9},{7,10},{8,11},{9,12},{10... | collective-permute-start | bytes 98312 | tf_op jit(solution)/shard_map/ppermute | solution.py:28
  134.2 26.9 %collective-permute-start.8 = (bf16[7,4,128,128]{2,3,1,0:T(8,128)(2,1)S(1)}, bf16[7,4,128,128]{2,3,1,0:T(8,128)(2,1)S(1)}, u32[]{:S(2)}, u32[]{:S(2)}) collective-permute-start(bf16[7,4,128,128]{2,3,1,0:T(8,128)(2,1)S(1)} %get-tuple-element.54), channel_id=1, source_target_pairs={{0,32},{32,64},{64,96},{96,128},{128,160},{160,192},{192,224},{224... | collective-permute-start | bytes 2752520 | tf_op jit(solution)/shard_map/ppermute | solution.py:15
  137.3 34.8 %collective-permute-start.9 = (bf16[7,4,128,128]{2,3,1,0:T(8,128)(2,1)S(1)}, bf16[7,4,128,128]{2,3,1,0:T(8,128)(2,1)}, u32[]{:S(2)}, u32[]{:S(2)}) collective-permute-start(bf16[7,4,128,128]{2,3,1,0:T(8,128)(2,1)S(1)} %get-tuple-element.54), channel_id=1, source_target_pairs={{0,480},{32,0},{64,32},{96,64},{128,96},{160,128},{192,160},{224,1... | collective-permute-start | bytes 2752520 | tf_op jit(solution)/shard_map/ppermute | solution.py:18
  161.1 26.1 %collective-permute-start.10 = (bf16[7,4,128,128]{2,3,1,0:T(8,128)(2,1)S(1)}, bf16[7,4,128,128]{2,3,1,0:T(8,128)(2,1)}, u32[]{:S(2)}, u32[]{:S(2)}) collective-permute-start(bf16[7,4,128,128]{2,3,1,0:T(8,128)(2,1)S(1)} %collective-permute-done.8), channel_id=1, source_target_pairs={{0,32},{32,64},{64,96},{96,128},{128,160},{160,192},{192,224},{224... | collective-permute-start | bytes 2752520 | tf_op jit(solution)/shard_map/ppermute | solution.py:15
  163.6 41.0 %collective-permute-start.31 = (bf16[1,128,128]{2,1,0:T(8,128)(2,1)S(1)}, bf16[1,128,128]{2,1,0:T(8,128)(2,1)S(1)}, u32[]{:S(2)}, u32[]{:S(2)}) collective-permute-start(bf16[1,128,128]{2,1,0:T(8,128)(2,1)S(1)} %get-tuple-element.59), channel_id=1, source_target_pairs={{0,1},{1,2},{2,3},{3,4},{4,5},{5,6},{6,7},{7,8},{8,9},{9,10},{10,1... | collective-permute-start | bytes 98312 | tf_op jit(solution)/shard_map/ppermute | solution.py:28
  167.7 39.0 %collective-permute-start.32 = (bf16[1,128,128]{2,1,0:T(8,128)(2,1)S(1)}, bf16[1,128,128]{2,1,0:T(8,128)(2,1)S(1)}, u32[]{:S(2)}, u32[]{:S(2)}) collective-permute-start(bf16[1,128,128]{2,1,0:T(8,128)(2,1)S(1)} %get-tuple-element.59), channel_id=1, source_target_pairs={{1,0},{2,1},{3,2},{4,3},{5,4},{6,5},{7,6},{8,7},{9,8},{10,9},{11,1... | collective-permute-start | bytes 98312 | tf_op jit(solution)/shard_map/ppermute | solution.py:28
  169.6 44.7 %collective-permute-start.33 = (bf16[1,128,128]{2,1,0:T(8,128)(2,1)S(1)}, bf16[1,128,128]{2,1,0:T(8,128)(2,1)S(1)}, u32[]{:S(2)}, u32[]{:S(2)}) collective-permute-start(bf16[1,128,128]{2,1,0:T(8,128)(2,1)S(1)} %get-tuple-element.59), channel_id=1, source_target_pairs={{0,2},{1,3},{2,4},{3,5},{4,6},{5,7},{6,8},{7,9},{8,10},{9,11},{10,... | collective-permute-start | bytes 98312 | tf_op jit(solution)/shard_map/ppermute | solution.py:28
  172.1 43.4 %collective-permute-start.11 = (bf16[7,4,128,128]{2,3,1,0:T(8,128)(2,1)}, bf16[7,4,128,128]{2,3,1,0:T(8,128)(2,1)}, u32[]{:S(2)}, u32[]{:S(2)}) collective-permute-start(bf16[7,4,128,128]{2,3,1,0:T(8,128)(2,1)} %collective-permute-done.9), channel_id=1, source_target_pairs={{0,480},{32,0},{64,32},{96,64},{128,96},{160,128},{192,160},{224,1... | collective-permute-start | bytes 2752520 | tf_op jit(solution)/shard_map/ppermute | solution.py:18
  187.1 35.4 %collective-permute-start.12 = (bf16[7,4,128,128]{2,3,1,0:T(8,128)(2,1)}, bf16[7,4,128,128]{2,3,1,0:T(8,128)(2,1)}, u32[]{:S(2)}, u32[]{:S(2)}) collective-permute-start(bf16[7,4,128,128]{2,3,1,0:T(8,128)(2,1)} %collective-permute-done.10), channel_id=1, source_target_pairs={{0,32},{32,64},{64,96},{96,128},{128,160},{160,192},{192,224},{224... | collective-permute-start | bytes 2752520 | tf_op jit(solution)/shard_map/ppermute | solution.py:15
  204.7 20.4 %collective-permute-start.34 = (bf16[1,128,128]{2,1,0:T(8,128)(2,1)S(1)}, bf16[1,128,128]{2,1,0:T(8,128)(2,1)S(1)}, u32[]{:S(2)}, u32[]{:S(2)}) collective-permute-start(bf16[1,128,128]{2,1,0:T(8,128)(2,1)S(1)} %get-tuple-element.59), channel_id=1, source_target_pairs={{2,0},{3,1},{4,2},{5,3},{6,4},{7,5},{8,6},{9,7},{10,8},{11,9},{12,... | collective-permute-start | bytes 98312 | tf_op jit(solution)/shard_map/ppermute | solution.py:28
  206.6 24.1 %collective-permute-start.35 = (bf16[1,128,128]{2,1,0:T(8,128)(2,1)S(1)}, bf16[1,128,128]{2,1,0:T(8,128)(2,1)S(1)}, u32[]{:S(2)}, u32[]{:S(2)}) collective-permute-start(bf16[1,128,128]{2,1,0:T(8,128)(2,1)S(1)} %get-tuple-element.59), channel_id=1, source_target_pairs={{0,3},{1,4},{2,5},{3,6},{4,7},{5,8},{6,9},{7,10},{8,11},{9,12},{10... | collective-permute-start | bytes 98312 | tf_op jit(solution)/shard_map/ppermute | solution.py:28
  214.2 18.4 %collective-permute-start.36 = (bf16[1,128,128]{2,1,0:T(8,128)(2,1)S(1)}, bf16[1,128,128]{2,1,0:T(8,128)(2,1)S(1)}, u32[]{:S(2)}, u32[]{:S(2)}) collective-permute-start(bf16[1,128,128]{2,1,0:T(8,128)(2,1)S(1)} %get-tuple-element.59), channel_id=1, source_target_pairs={{3,0},{4,1},{5,2},{6,3},{7,4},{8,5},{9,6},{10,7},{11,8},{12,9},{13... | collective-permute-start | bytes 98312 | tf_op jit(solution)/shard_map/ppermute | solution.py:28
  215.5 29.4 %collective-permute-start.13 = (bf16[7,4,128,128]{2,3,1,0:T(8,128)(2,1)}, bf16[7,4,128,128]{2,3,1,0:T(8,128)(2,1)S(1)}, u32[]{:S(2)}, u32[]{:S(2)}) collective-permute-start(bf16[7,4,128,128]{2,3,1,0:T(8,128)(2,1)} %collective-permute-done.11), channel_id=1, source_target_pairs={{0,480},{32,0},{64,32},{96,64},{128,96},{160,128},{192,160},{224,1... | collective-permute-start | bytes 2752520 | tf_op jit(solution)/shard_map/ppermute | solution.py:18
  222.5 29.4 %collective-permute-start.14 = (bf16[7,4,128,128]{2,3,1,0:T(8,128)(2,1)}, bf16[7,4,128,128]{2,3,1,0:T(8,128)(2,1)S(1)}, u32[]{:S(2)}, u32[]{:S(2)}) collective-permute-start(bf16[7,4,128,128]{2,3,1,0:T(8,128)(2,1)} %collective-permute-done.12), channel_id=1, source_target_pairs={{0,32},{32,64},{64,96},{96,128},{128,160},{160,192},{192,224},{224... | collective-permute-start | bytes 2752520 | tf_op jit(solution)/shard_map/ppermute | solution.py:15
  232.6 21.9 %collective-permute-start.23 = (bf16[1,128,128]{2,1,0:T(8,128)(2,1)S(1)}, bf16[1,128,128]{2,1,0:T(8,128)(2,1)S(1)}, u32[]{:S(2)}, u32[]{:S(2)}) collective-permute-start(bf16[1,128,128]{2,1,0:T(8,128)(2,1)S(1)} %get-tuple-element.61), channel_id=1, source_target_pairs={{0,1},{1,2},{2,3},{3,4},{4,5},{5,6},{6,7},{7,8},{8,9},{9,10},{10,1... | collective-permute-start | bytes 98312 | tf_op jit(solution)/shard_map/ppermute | solution.py:28
  236.2 19.5 %collective-permute-start.24 = (bf16[1,128,128]{2,1,0:T(8,128)(2,1)S(1)}, bf16[1,128,128]{2,1,0:T(8,128)(2,1)S(1)}, u32[]{:S(2)}, u32[]{:S(2)}) collective-permute-start(bf16[1,128,128]{2,1,0:T(8,128)(2,1)S(1)} %get-tuple-element.61), channel_id=1, source_target_pairs={{1,0},{2,1},{3,2},{4,3},{5,4},{6,5},{7,6},{8,7},{9,8},{10,9},{11,1... | collective-permute-start | bytes 98312 | tf_op jit(solution)/shard_map/ppermute | solution.py:28
  238.8 23.3 %collective-permute-start.25 = (bf16[1,128,128]{2,1,0:T(8,128)(2,1)S(1)}, bf16[1,128,128]{2,1,0:T(8,128)(2,1)S(1)}, u32[]{:S(2)}, u32[]{:S(2)}) collective-permute-start(bf16[1,128,128]{2,1,0:T(8,128)(2,1)S(1)} %get-tuple-element.61), channel_id=1, source_target_pairs={{0,2},{1,3},{2,4},{3,5},{4,6},{5,7},{6,8},{7,9},{8,10},{9,11},{10,... | collective-permute-start | bytes 98312 | tf_op jit(solution)/shard_map/ppermute | solution.py:28
  244.9 28.6 %collective-permute-start.15 = (bf16[7,4,128,128]{2,3,1,0:T(8,128)(2,1)S(1)}, bf16[7,4,128,128]{2,3,1,0:T(8,128)(2,1)S(1)}, u32[]{:S(2)}, u32[]{:S(2)}) collective-permute-start(bf16[7,4,128,128]{2,3,1,0:T(8,128)(2,1)S(1)} %collective-permute-done.13), channel_id=1, source_target_pairs={{0,480},{32,0},{64,32},{96,64},{128,96},{160,128},{192,160},{224,1... | collective-permute-start | bytes 2752520 | tf_op jit(solution)/shard_map/ppermute | solution.py:18
  251.9 28.6 %collective-permute-start.16 = (bf16[7,4,128,128]{2,3,1,0:T(8,128)(2,1)S(1)}, bf16[7,4,128,128]{2,3,1,0:T(8,128)(2,1)S(1)}, u32[]{:S(2)}, u32[]{:S(2)}) collective-permute-start(bf16[7,4,128,128]{2,3,1,0:T(8,128)(2,1)S(1)} %collective-permute-done.14), channel_id=1, source_target_pairs={{0,32},{32,64},{64,96},{96,128},{128,160},{160,192},{192,224},{224... | collective-permute-start | bytes 2752520 | tf_op jit(solution)/shard_map/ppermute | solution.py:15
  262.1 20.4 %collective-permute-start.28 = (bf16[1,128,128]{2,1,0:T(8,128)(2,1)S(1)}, bf16[1,128,128]{2,1,0:T(8,128)(2,1)S(1)}, u32[]{:S(2)}, u32[]{:S(2)}) collective-permute-start(bf16[1,128,128]{2,1,0:T(8,128)(2,1)S(1)} %get-tuple-element.61), channel_id=1, source_target_pairs={{3,0},{4,1},{5,2},{6,3},{7,4},{8,5},{9,6},{10,7},{11,8},{12,9},{13... | collective-permute-start | bytes 98312 | tf_op jit(solution)/shard_map/ppermute | solution.py:28
  263.4 19.1 %collective-permute-start.29 = (bf16[1,128,128]{2,1,0:T(8,128)(2,1)S(1)}, bf16[1,128,128]{2,1,0:T(8,128)(2,1)S(1)}, u32[]{:S(2)}, u32[]{:S(2)}) collective-permute-start(bf16[1,128,128]{2,1,0:T(8,128)(2,1)S(1)} %get-tuple-element.61), channel_id=1, source_target_pairs={{0,4},{1,5},{2,6},{3,7},{4,8},{5,9},{6,10},{7,11},{8,12},{9,13},{1... | collective-permute-start | bytes 98312 | tf_op jit(solution)/shard_map/ppermute | solution.py:28
  273.6 24.3 %collective-permute-start.17 = (bf16[7,4,128,128]{2,3,1,0:T(8,128)(2,1)S(1)}, bf16[7,4,128,128]{2,3,1,0:T(8,128)(2,1)S(1)}, u32[]{:S(2)}, u32[]{:S(2)}) collective-permute-start(bf16[7,4,128,128]{2,3,1,0:T(8,128)(2,1)S(1)} %collective-permute-done.15), channel_id=1, source_target_pairs={{0,480},{32,0},{64,32},{96,64},{128,96},{160,128},{192,160},{224,1... | collective-permute-start | bytes 2752520 | tf_op jit(solution)/shard_map/ppermute | solution.py:18
  280.6 25.8 %collective-permute-start.18 = (bf16[7,4,128,128]{2,3,1,0:T(8,128)(2,1)S(1)}, bf16[7,4,128,128]{2,3,1,0:T(8,128)(2,1)S(1)}, u32[]{:S(2)}, u32[]{:S(2)}) collective-permute-start(bf16[7,4,128,128]{2,3,1,0:T(8,128)(2,1)S(1)} %collective-permute-done.16), channel_id=1, source_target_pairs={{0,32},{32,64},{64,96},{96,128},{128,160},{160,192},{192,224},{224... | collective-permute-start | bytes 2752520 | tf_op jit(solution)/shard_map/ppermute | solution.py:15
  297.9 25.6 %collective-permute-start.19 = (bf16[7,4,128,128]{2,3,1,0:T(8,128)(2,1)S(1)}, bf16[7,4,128,128]{2,3,1,0:T(8,128)(2,1)S(1)}, u32[]{:S(2)}, u32[]{:S(2)}) collective-permute-start(bf16[7,4,128,128]{2,3,1,0:T(8,128)(2,1)S(1)} %collective-permute-done.17), channel_id=1, source_target_pairs={{0,480},{32,0},{64,32},{96,64},{128,96},{160,128},{192,160},{224,1... | collective-permute-start | bytes 2752520 | tf_op jit(solution)/shard_map/ppermute | solution.py:18
  306.3 25.9 %collective-permute-start.20 = (bf16[7,4,128,128]{2,3,1,0:T(8,128)(2,1)S(1)}, bf16[7,4,128,128]{2,3,1,0:T(8,128)(2,1)S(1)}, u32[]{:S(2)}, u32[]{:S(2)}) collective-permute-start(bf16[7,4,128,128]{2,3,1,0:T(8,128)(2,1)S(1)} %collective-permute-done.18), channel_id=1, source_target_pairs={{0,32},{32,64},{64,96},{96,128},{128,160},{160,192},{192,224},{224... | collective-permute-start | bytes 2752520 | tf_op jit(solution)/shard_map/ppermute | solution.py:15
  323.5 26.7 %collective-permute-start.21 = (bf16[7,4,128,128]{2,3,1,0:T(8,128)(2,1)S(1)}, bf16[7,4,128,128]{2,3,1,0:T(8,128)(2,1)S(1)}, u32[]{:S(2)}, u32[]{:S(2)}) collective-permute-start(bf16[7,4,128,128]{2,3,1,0:T(8,128)(2,1)S(1)} %collective-permute-done.19), channel_id=1, source_target_pairs={{0,480},{32,0},{64,32},{96,64},{128,96},{160,128},{192,160},{224,1... | collective-permute-start | bytes 2752520 | tf_op jit(solution)/shard_map/ppermute | solution.py:18
  332.2 27.0 %collective-permute-start.22 = (bf16[7,4,128,128]{2,3,1,0:T(8,128)(2,1)S(1)}, bf16[7,4,128,128]{2,3,1,0:T(8,128)(2,1)S(1)}, u32[]{:S(2)}, u32[]{:S(2)}) collective-permute-start(bf16[7,4,128,128]{2,3,1,0:T(8,128)(2,1)S(1)} %collective-permute-done.20), channel_id=1, source_target_pairs={{0,32},{32,64},{64,96},{96,128},{128,160},{160,192},{192,224},{224... | collective-permute-start | bytes 2752520 | tf_op jit(solution)/shard_map/ppermute | solution.py:15
  (15 other events, 980.8 us)
Sparse Core Ops, SparseCore 0:
  46.8 74.5 all-gather.1
